TPU v7x, 256 devices: a whole 4x4x8 slice. The times are simulated.
256 devices in a mesh: row: 32 (over y, x, z_hi), col: 8 (over z_lo, core).
Axes of the slice: x: 4, y: 4, z: 8 (z_hi: 2, z_lo: 4; z = z_hi * 4 + z_lo), core: 2. Of those that a mesh axis runs over, the one named last changes fastest.
Arguments:
- alignment: bfloat16 [64, 1536, 256], P('row', 'col'), may hold values from -6 to 6
- pair_act: bfloat16 [1536, 1536, 128], P('row', 'col'), may hold values from -600 to 600
- targets: int32 [1536, 1536], P('row', 'col'), may hold values from 0 to 63, as said below
- crop_mask: int32 [1536], replicated, may hold values 0 or 1
- projection_weight: bfloat16 [256, 64], replicated, may hold values from -0.375 to 0.375
- w_outer: bfloat16 [1024, 128], replicated, may hold values from -1.5 to 1.5
- w_expand: bfloat16 [128, 512], replicated, may hold values from -0.5 to 0.5
- w_shrink: bfloat16 [512, 128], replicated, may hold values from -0.25 to 0.25
- w_bins: bfloat16 [128, 64], replicated, may hold values from -1.8 to 1.8
Outputs:
- pair_grad: bfloat16 [1536, 1536, 128], P('row', 'col')
Inputs may be any that keep to these rules, and one draw needn't show every extreme that they name: targets[i, j] equals targets[j, i].
All inputs are finite; a program needn't handle non-finite values.
Results may differ from a plain program's by a relative error of at most 0.02.
The roundings to bfloat16 on the way count: a program that leaves them out, or rounds other values in their place, can miss the bound.
Values may be sent and summed in bfloat16 or wider, within the bound.
A program may use at most 128 MiB of HBM per device.

v0:
```python
import jax
import jax.numpy as jnp
from jax import lax
from jax.sharding import PartitionSpec as P

FACTOR_CHANNELS = 32
BINS = 64
SEQUENCE_COUNT = 64
epsilon = 1e-05


def from_root(shard, axis, root):
    mine = lax.axis_index(axis) == root
    return lax.psum(jnp.where(mine, shard, jnp.zeros_like(shard)), axis)


def layer_normalize(values):
    average = jnp.mean(values, axis=-1, keepdims=True)
    centred = values - average
    inverse_deviation = lax.rsqrt(jnp.mean(centred * centred, axis=-1, keepdims=True) + epsilon)
    return (centred * inverse_deviation, inverse_deviation)


def norm_project(shard_rows, projection_weight):
    normed = layer_normalize(shard_rows.astype(jnp.float32))[0].astype(jnp.bfloat16)
    factor = jnp.dot(normed, projection_weight, preferred_element_type=jnp.float32).astype(
        jnp.bfloat16
    )
    return factor.reshape(shard_rows.shape[0], -1)


def mirrored(tile_rows, rows_dev, n_row, n_col):
    ratio = n_row // n_col
    group_rows = tile_rows.shape[0] // n_col
    sectioned = tile_rows.reshape(n_col, group_rows, ratio, rows_dev * BINS).transpose(0, 2, 1, 3)
    first_hop = lax.all_to_all(sectioned, "col", split_axis=0, concat_axis=0, tiled=True)
    regrouped = first_hop.reshape(n_row, 1, group_rows, rows_dev * BINS)
    arrived = lax.all_to_all(
        lax.all_to_all(regrouped, "row", split_axis=0, concat_axis=1, tiled=True),
        "col",
        split_axis=1,
        concat_axis=0,
        tiled=True,
    )
    return arrived.reshape(n_col, ratio, group_rows, rows_dev, BINS).transpose(3, 1, 0, 2, 4)


def per_device(
    alignment, pair_act, targets, crop_mask, projection_weight, w_outer, w_expand, w_shrink, w_bins
):
    rows_dev, cols_dev, channels = pair_act.shape
    n_row = lax.axis_size("row")
    n_col = lax.axis_size("col")
    ratio = n_row // n_col
    row_index = lax.axis_index("row")
    col_index = lax.axis_index("col")
    factors = norm_project(lax.all_gather(alignment, "row", axis=0, tiled=True), projection_weight)
    factors = factors.reshape(SEQUENCE_COUNT, cols_dev, 2 * FACTOR_CHANNELS)
    right_side = factors[:, :, FACTOR_CHANNELS:]
    own_left = lax.dynamic_slice_in_dim(
        factors[:, :, :FACTOR_CHANNELS], row_index % ratio * rows_dev, rows_dev, 1
    )
    left_side = from_root(
        own_left.reshape(SEQUENCE_COUNT, rows_dev * FACTOR_CHANNELS), "col", row_index // ratio
    )
    left_side = left_side.reshape(SEQUENCE_COUNT, rows_dev, FACTOR_CHANNELS)
    block_rows = 8
    blocks = rows_dev // block_rows
    pair_blocks = pair_act.reshape(blocks, block_rows, cols_dev, channels)
    left_blocks = left_side.reshape(SEQUENCE_COUNT, blocks, block_rows, FACTOR_CHANNELS).transpose(
        1, 0, 2, 3
    )

    def forward_block(inputs):
        pair_rows, left_rows = inputs
        outer = (
            jnp.einsum("sic,sje->ijce", left_rows, right_side, preferred_element_type=jnp.float32)
            / SEQUENCE_COUNT
        )
        outer = outer.reshape(block_rows * cols_dev, FACTOR_CHANNELS * FACTOR_CHANNELS).astype(
            jnp.bfloat16
        )
        update = jnp.dot(outer, w_outer, preferred_element_type=jnp.float32)
        middle_state = (
            pair_rows.reshape(block_rows * cols_dev, channels).astype(jnp.float32) + update
        ).astype(jnp.bfloat16)
        xnorm = layer_normalize(middle_state.astype(jnp.float32))[0].astype(jnp.bfloat16)
        before = lax.optimization_barrier(
            jnp.dot(xnorm, w_expand, preferred_element_type=jnp.float32).astype(jnp.bfloat16)
        )
        hidden = jax.nn.silu(before.astype(jnp.float32)).astype(jnp.bfloat16)
        final = (
            middle_state.astype(jnp.float32)
            + jnp.dot(hidden, w_shrink, preferred_element_type=jnp.float32)
        ).astype(jnp.bfloat16)
        logits = jnp.dot(final, w_bins, preferred_element_type=jnp.float32).astype(jnp.bfloat16)
        return (middle_state, before, logits.reshape(block_rows, cols_dev * BINS))

    middle_state, before, logits = lax.map(forward_block, (pair_blocks, left_blocks))
    across = mirrored(logits.reshape(rows_dev, cols_dev * BINS), rows_dev, n_row, n_col).reshape(
        rows_dev, cols_dev, BINS
    )
    own = logits.reshape(rows_dev, cols_dev, BINS)
    scores = own.astype(jnp.float32) + across.astype(jnp.float32)
    scores = scores - jnp.max(scores, axis=-1, keepdims=True)
    expo = jnp.exp(scores)
    prob = expo / jnp.sum(expo, axis=-1, keepdims=True)
    onehot = (targets[:, :, None] == jnp.arange(BINS, dtype=jnp.int32)).astype(jnp.float32)
    row_mask = lax.dynamic_slice_in_dim(crop_mask, row_index * rows_dev, rows_dev).astype(
        jnp.float32
    )
    col_mask = lax.dynamic_slice_in_dim(crop_mask, col_index * cols_dev, cols_dev).astype(
        jnp.float32
    )
    weight = row_mask[:, None] * col_mask[None, :]
    dlogits = (2.0 * (prob - onehot) * weight[:, :, None]).astype(jnp.bfloat16)
    dlog_blocks = dlogits.reshape(blocks, block_rows * cols_dev, BINS)

    def backward_block(inputs):
        middle_row_block, before_rows, dlog_rows = inputs
        final_gradient = jnp.dot(dlog_rows, w_bins.T, preferred_element_type=jnp.float32)
        before_f = before_rows.astype(jnp.float32)
        sigma = jax.nn.sigmoid(before_f)
        slope = sigma * (1.0 + before_f * (1.0 - sigma))
        dhidden = (
            jnp.dot(
                final_gradient.astype(jnp.bfloat16), w_shrink.T, preferred_element_type=jnp.float32
            )
            * slope
        ).astype(jnp.bfloat16)
        normed_input_gradient = jnp.dot(dhidden, w_expand.T, preferred_element_type=jnp.float32)
        standardized_input, inverse_deviation = layer_normalize(
            middle_row_block.astype(jnp.float32)
        )
        middle_gradient = final_gradient + inverse_deviation * (
            normed_input_gradient
            - jnp.mean(normed_input_gradient, axis=-1, keepdims=True)
            - standardized_input
            * jnp.mean(normed_input_gradient * standardized_input, axis=-1, keepdims=True)
        )
        return middle_gradient.astype(jnp.bfloat16)

    grads = lax.map(backward_block, (middle_state, before, dlog_blocks))
    return grads.reshape(rows_dev, cols_dev, channels)


def solution(mesh):
    in_specs = (
        P("row", "col", None),
        P("row", "col", None),
        P("row", "col"),
        P(),
        P(),
        P(),
        P(),
        P(),
        P(),
    )
    out_specs = P("row", "col", None)
    return jax.shard_map(
        per_device, mesh=mesh, in_specs=in_specs, out_specs=out_specs, check_vma=False
    )
```

profile of v0, /device:TPU:1, one launch (start us, length us, event | category | flops | bytes accessed | tf_op | source)
XLA Modules:
  0.0 618.3 jit_solution(1737578397463702173)
XLA Ops:
  7.3 138.0 %all-gather.2.cloned.1.call-done = bf16[64,192,256]{2,1,0:T(8,128)(2,1)} async-done(((bf16[2,192,256]{2,1,0:T(8,128)(2,1)}), bf16[64,192,256]{2,1,0:T(8,128)(2,1)}) %all-gather.2.cloned.1.call-update) | async-done | bytes 6291472 | tf_op jit(solution)/shard_map/all_gather | solution.py:57
  145.3 5.2 convert_reduce_fusion.2
  150.5 4.4 fusion.54
  155.0 5.2 fusion.60
  164.0 62.7 %all-reduce.2.cloned.1.call-done = bf16[6,64,8,32]{1,3,2,0:T(8,128)(2,1)} async-done(((bf16[6,64,8,32]{1,3,2,0:T(8,128)(2,1)}), bf16[6,64,8,32]{1,3,2,0:T(8,128)(2,1)}) %all-reduce.2.cloned.1.call-update) | async-done | bytes 196624 | tf_op jit(solution)/shard_map/psum | solution.py:14
  226.7 158.3 %while.24 = (s32[]{:T(128)}, bf16[6,1536,128]{1,2,0:T(8,128)(2,1)}, bf16[6,1536,512]{2,1,0:T(8,128)(2,1)}, bf16[6,8,12288]{2,1,0:T(8,128)(2,1)}, bf16[6,8,192,12...) while((s32[]{:T(128)}, bf16[6,1536,128]{1,2,0:T(8,128)(2,1)}, ...), condition=%wide.region_6.7_spmd, body=%wide.region_3.6_spmd.sunk | while | flops 1043695104 | bytes 37036208 | solution.py:99
  226.7 2.5 fusion.107
  229.2 4.5 copy.80
  233.7 6.3 %convert_element_type.284 = bf16[1536,1024]{0,1:T(8,128)(2,1)S(1)} reshape(bf16[8,192,32,32]{1,0,3,2:T(8,128)(2,1)} %copy.80) | data formatting | bytes 6291456 | tf_op jit(solution)/shard_map/while/body/eval_jaxpr/convert_element_type | solution.py:80
  242.0 2.3 copy.79
  244.3 2.6 bitcast_dynamic-update-slice_fusion.4
  248.3 2.3 convolution_convert_fusion.5
  253.1 2.5 fusion.107
  255.6 4.5 copy.80
  260.1 6.3 %convert_element_type.284 = bf16[1536,1024]{0,1:T(8,128)(2,1)S(1)} reshape(bf16[8,192,32,32]{1,0,3,2:T(8,128)(2,1)} %copy.80) | data formatting | bytes 6291456 | tf_op jit(solution)/shard_map/while/body/eval_jaxpr/convert_element_type | solution.py:80
  268.4 2.3 copy.79
  270.7 2.6 bitcast_dynamic-update-slice_fusion.4
  274.6 2.3 convolution_convert_fusion.5
  279.5 2.5 fusion.107
  282.0 4.5 copy.80
  286.5 6.3 %convert_element_type.284 = bf16[1536,1024]{0,1:T(8,128)(2,1)S(1)} reshape(bf16[8,192,32,32]{1,0,3,2:T(8,128)(2,1)} %copy.80) | data formatting | bytes 6291456 | tf_op jit(solution)/shard_map/while/body/eval_jaxpr/convert_element_type | solution.py:80
  294.8 2.3 copy.79
  297.1 2.6 bitcast_dynamic-update-slice_fusion.4
  301.0 2.3 convolution_convert_fusion.5
  305.9 2.5 fusion.107
  308.3 4.5 copy.80
  312.8 6.3 %convert_element_type.284 = bf16[1536,1024]{0,1:T(8,128)(2,1)S(1)} reshape(bf16[8,192,32,32]{1,0,3,2:T(8,128)(2,1)} %copy.80) | data formatting | bytes 6291456 | tf_op jit(solution)/shard_map/while/body/eval_jaxpr/convert_element_type | solution.py:80
  321.1 2.3 copy.79
  323.4 2.6 bitcast_dynamic-update-slice_fusion.4
  327.3 2.3 convolution_convert_fusion.5
  332.2 2.5 fusion.107
  334.7 4.5 copy.80
  339.2 6.3 %convert_element_type.284 = bf16[1536,1024]{0,1:T(8,128)(2,1)S(1)} reshape(bf16[8,192,32,32]{1,0,3,2:T(8,128)(2,1)} %copy.80) | data formatting | bytes 6291456 | tf_op jit(solution)/shard_map/while/body/eval_jaxpr/convert_element_type | solution.py:80
  347.5 2.3 copy.79
  349.8 2.5 bitcast_dynamic-update-slice_fusion.4
  353.7 2.3 convolution_convert_fusion.5
  358.6 2.5 fusion.107
  361.1 4.5 copy.80
  365.6 6.3 %convert_element_type.284 = bf16[1536,1024]{0,1:T(8,128)(2,1)S(1)} reshape(bf16[8,192,32,32]{1,0,3,2:T(8,128)(2,1)} %copy.80) | data formatting | bytes 6291456 | tf_op jit(solution)/shard_map/while/body/eval_jaxpr/convert_element_type | solution.py:80
  373.9 2.3 copy.79
  376.1 2.6 bitcast_dynamic-update-slice_fusion.4
  380.1 2.3 convolution_convert_fusion.5
  385.0 2.0 reshape_reshape.7
  387.0 34.3 %all_to_all.26 = bf16[8,4,6,3072]{3,1,2,0:T(4,128)(2,1)S(1)} all-to-all(bf16[8,4,6,3072]{3,1,2,0:T(4,128)(2,1)S(1)} %bitcast.140), channel_id=1, replica_groups=mesh['row'=32,'col'=8] {'col'}, dimensions={0} | all-to-all | bytes 2359296 | tf_op jit(solution)/shard_map/all_to_all | solution.py:36
  421.7 50.7 %all_to_all.27 = bf16[32,1,6,3072]{3,2,1,0:T(8,128)(2,1)} all-to-all(bf16[32,1,6,3072]{3,2,1,0:T(8,128)(2,1)S(1)} %bitcast.139), channel_id=1, replica_groups=mesh['row'=32,'col'=8] {'row'}, dimensions={0} | all-to-all | bytes 2359296 | tf_op jit(solution)/shard_map/all_to_all | solution.py:39
  472.4 7.7 %all-to-all-start.2 = ((bf16[1,32,6,3072]{3,2,0,1:T(8,128)(2,1)}), bf16[1,32,6,3072]{3,2,0,1:T(8,128)(2,1)}, u32[]{:S(2)}, u32[]{:S(2)}) async-start(bf16[1,32,6,3072]{3,2,0,1:T(8,128)(2,1)} %bitcast.20), calls=%async_computation.2 | async-start | bytes 3145728 | tf_op jit(solution)/shard_map/all_to_all | solution.py:38
  482.1 3.6 reshape.139
  485.8 3.5 reshape.137
  489.3 27.8 %all-to-all-done.2 = bf16[1,32,6,3072]{3,2,0,1:T(8,128)(2,1)} async-done(((bf16[1,32,6,3072]{3,2,0,1:T(8,128)(2,1)}), bf16[1,32,6,3072]{3,2,0,1:T(8,128)(2,1)}, u32[]{:S(2)}, u32[]{:S(2)}) %all-to-all-start.2) | async-done | bytes 1179680 | tf_op jit(solution)/shard_map/all_to_all | solution.py:38
  517.1 2.1 copy_convert_fusion
  519.2 3.2 reshape.141
  522.4 3.0 copy.60
  526.1 2.4 fusion.63
  528.6 4.7 exponential_reduce_fusion
  533.3 7.9 %copy.59 = f32[48,4,8,6,64]{4,3,2,1,0:T(8,128)} copy(f32[48,4,8,6,64]{4,0,1,2,3:T(8,128)} %bitcast.138) | data formatting | bytes 4718592 | tf_op jit(solution)/shard_map/convert_element_type | solution.py:104
  541.3 6.6 %reshape.138 = f32[6,1536,64]{2,1,0:T(8,128)} reshape(f32[48,4,8,6,64]{4,3,2,1,0:T(8,128)} %copy.59) | data formatting | bytes 4718592 | tf_op jit(solution)/shard_map/convert_element_type | solution.py:104
  547.9 8.4 %multiply_convert_fusion.1 = bf16[6,1536,64]{2,1,0:T(8,128)(2,1)} fusion(f32[6,1536,64]{2,1,0:T(8,128)} %reshape.137, f32[6,1536,64]{2,1,0:T(8,128)} %reshape.138, f32[6,1536]{1,0:T(8,128)S(1)} %multiply_multiply_fusion, s32[6,1536]{1,0:T(8,128)S(1)} %eq.22, f32[6,1536]{1,0:T(8,128)S(1)} %div.58, f32[6,1536]{1,0:T(8,128)S(1)} %sub.64), kind=kLoop, calls=%fused_computation.82 | loop fusion | flops 4718592 | bytes 6045696 | tf_op jit(solution)/shard_map/convert_element_type | solution.py:116
  556.3 54.4 %while.25 = (s32[]{:T(128)}, bf16[6,1536,128]{2,1,0:T(8,128)(2,1)}, bf16[6,1536,64]{2,1,0:T(8,128)(2,1)}, bf16[128,64]{0,1:T(8,128)(2,1)S(1)}, bf16[6,1536,128]{...) while((s32[]{:T(128)}, bf16[6,1536,128]{2,1,0:T(8,128)(2,1)}, ...), condition=%wide.region_14.15_spmd, body=%wide.region_9.14_spmd.sunk | while | flops 440010240 | bytes 12193377 | solution.py:143
  559.8 2.9 fusion.115
  568.8 3.0 fusion.115
  577.8 2.9 fusion.115
  586.8 3.0 fusion.115
  595.8 2.9 fusion.115
  604.8 3.0 fusion.115
  (205 shorter events, 79.7 us)
Async XLA Ops:
  6.5 148.5 %copy-start = (bf16[256,64]{0,1:T(8,128)(2,1)S(1)}, bf16[256,64]{0,1:T(8,128)(2,1)}, u32[]{:S(2)}) copy-start(bf16[256,64]{0,1:T(8,128)(2,1)} %param.17) | copy-start | bytes 98308
  6.5 138.8 %all-gather.2.cloned.1.call-start = ((), (), s32[]{:S(2)}) async-start(), calls=%async_computation.3 | async-start | bytes 6488064 | tf_op jit(solution)/shard_map/all_gather | solution.py:57
  7.3 219.5 %all-reduce.2.cloned.1.call-start = ((), (), s32[]{:S(2)}) async-start(), calls=%async_computation.4 | async-start | bytes 786432 | tf_op jit(solution)/shard_map/psum | solution.py:14
  145.3 5.2 copy-start.3
  160.4 66.3 %copy-start.5 = (bf16[1024,128]{1,0:T(8,128)(2,1)S(1)}, bf16[1024,128]{1,0:T(8,128)(2,1)}, u32[]{:S(2)}) copy-start(bf16[1024,128]{1,0:T(8,128)(2,1)} %param.18) | copy-start | bytes 786436
  160.4 66.3 %copy-start.8 = (bf16[128,64]{0,1:T(8,128)(2,1)S(1)}, bf16[128,64]{0,1:T(8,128)(2,1)}, u32[]{:S(2)}) copy-start(bf16[128,64]{0,1:T(8,128)(2,1)} %param.21) | copy-start | bytes 49156
  244.3 3.3 copy-start.6
  246.9 0.7 copy-start.2
  270.7 3.3 copy-start.6
  273.3 0.7 copy-start.2
  297.1 3.3 copy-start.6
  299.6 0.7 copy-start.2
  323.4 3.3 copy-start.6
  326.0 0.7 copy-start.2
  349.8 3.3 copy-start.6
  352.4 0.7 copy-start.2
  376.1 3.3 copy-start.6
  378.7 0.7 copy-start.2
  421.7 60.3 %copy-start.9 = (s32[48,192]{1,0:T(8,128)S(1)}, s32[48,192]{1,0:T(8,128)}, u32[]{:S(2)}) copy-start(s32[48,192]{1,0:T(8,128)} %param.15) | copy-start | bytes 110596
  421.7 60.4 %copy-start.4 = (bf16[6,8,12288]{2,1,0:T(8,128)(2,1)S(1)}, bf16[6,8,12288]{2,1,0:T(8,128)(2,1)}, u32[]{:S(2)}) copy-start(bf16[6,8,12288]{2,1,0:T(8,128)(2,1)} %get-tuple-element.106) | copy-start | bytes 3538948
  472.4 44.7 %all-to-all-start.2 = ((bf16[1,32,6,3072]{3,2,0,1:T(8,128)(2,1)}), bf16[1,32,6,3072]{3,2,0,1:T(8,128)(2,1)}, u32[]{:S(2)}, u32[]{:S(2)}) async-start(bf16[1,32,6,3072]{3,2,0,1:T(8,128)(2,1)} %bitcast.20), calls=%async_computation.2 | async-start | bytes 3145728 | tf_op jit(solution)/shard_map/all_to_all | solution.py:38
  522.4 3.6 slice-start
  522.4 3.7 slice-start.1
  547.9 8.4 %copy-start.7 = (bf16[128,512]{1,0:T(8,128)(2,1)S(1)}, bf16[128,512]{1,0:T(8,128)(2,1)}, u32[]{:S(2)}) copy-start(bf16[128,512]{1,0:T(8,128)(2,1)} %get-tuple-element.426) | copy-start | bytes 393220
  547.9 8.4 %copy-start.10 = (bf16[512,128]{1,0:T(8,128)(2,1)S(1)}, bf16[512,128]{1,0:T(8,128)(2,1)}, u32[]{:S(2)}) copy-start(bf16[512,128]{1,0:T(8,128)(2,1)} %get-tuple-element.433) | copy-start | bytes 393220
  610.7 0.8 copy-start.1
Sparse Core Ops, SparseCore 0:
  10.8 134.4 all-gather.1
  162.5 64.1 all-reduce.1
where the time goes:
time: 621 us; the launch traced here: 618 us
  waiting for transfers between devices  229 us (37%)
  local copies, waits for them, and re-layouts  148 us (24%)
  blocking collectives  85 us (14%)
  matrix products  78 us (13%)
  other arithmetic  55.8 us (9%)
  between operations  13.7 us (2%)
  starting transfers between devices  7.75 us (1%)
    all_gather x1, waiting for transfers between devices, per_device(): lax.all_gather(alignment, 'row', axis=0, tiled=True)  138 us
    convert_element_type x12, local copies, waits for them, and re-layouts, forward_block(): outer.reshape(block_rows * cols_dev, FACTOR_CHANNELS * FACTOR_CHANNELS)  64.8 us
    psum x1, waiting for transfers between devices, from_root(): return lax.psum(jnp.where(mine, shard, jnp.zeros_like(shard)), axis)  62.7 us
    all_to_all x1, blocking collectives, mirrored(): lax.all_to_all(regrouped, 'row', split_axis=0, concat_axis=1, tiled=True)  50.7 us
    all_to_all x1, blocking collectives, mirrored(): lax.all_to_all(sectioned, 'col', split_axis=0, concat_axis=0, tiled=True)  34.3 us
    convert_element_type x6, local copies, waits for them, and re-layouts, per_device(): scores = own.astype(jnp.float32) + across.astype(jnp.float32)  27.8 us
    all_to_all x1, waiting for transfers between devices, mirrored(): lax.all_to_all(lax.all_to_all(regrouped, 'row', split_axis=0, concat_axis...  27.8 us
    dot_general x6, matrix products, backward_block(): jnp.dot(dhidden, w_expand.T, preferred_element_type=jnp.float32)  17.7 us
  transfers between devices with their start and end apart: 3, of which 3 were waited for; matrix products, arithmetic and copies ran while one was open for 2% of the time, Pallas kernels for 0%

commit v1 on v0

--- a/solution.py
+++ b/solution.py
@@ -11,7 +11,7 @@
 
 def from_root(shard, axis, root):
     mine = lax.axis_index(axis) == root
-    return lax.psum(jnp.where(mine, shard, jnp.zeros_like(shard)), axis)
+    return jnp.sum(lax.all_gather(jnp.where(mine, shard, jnp.zeros_like(shard)), axis), axis=0)
 
 
 def layer_normalize(values):

time: 621 us -> 590 us (0.950)
  waiting for transfers between devices: 229 us -> 196 us
    psum x1 -> x0, waiting for transfers between devices: 62.7 us -> none  [from_root(): return lax.psum(jnp.where(mine, shard, jnp.zeros_like(shard)), axis)]
    all_gather x0 -> x1, waiting for transfers between devices: none -> 29.6 us  [from_root(): lax.all_gather(jnp.where(mine, shard, jnp.zeros_like(shard)), axis)]
where the time goes in v1:
time: 590 us; the launch traced here: 587 us
  waiting for transfers between devices  196 us (33%)
  local copies, waits for them, and re-layouts  149 us (25%)
  blocking collectives  84.7 us (14%)
  matrix products  78 us (13%)
  other arithmetic  57.4 us (10%)
  between operations  13.7 us (2%)
  starting transfers between devices  7.75 us (1%)
    all_gather x1, waiting for transfers between devices, per_device(): lax.all_gather(alignment, 'row', axis=0, tiled=True)  138 us
    convert_element_type x12, local copies, waits for them, and re-layouts, forward_block(): outer.reshape(block_rows * cols_dev, FACTOR_CHANNELS * FACTOR_CHANNELS)  64.8 us
    all_to_all x1, blocking collectives, mirrored(): lax.all_to_all(regrouped, 'row', split_axis=0, concat_axis=1, tiled=True)  50.7 us
    all_to_all x1, blocking collectives, mirrored(): lax.all_to_all(sectioned, 'col', split_axis=0, concat_axis=0, tiled=True)  34 us
    all_gather x1, waiting for transfers between devices, from_root(): lax.all_gather(jnp.where(mine, shard, jnp.zeros_like(shard)), axis)  29.6 us
    convert_element_type x6, local copies, waits for them, and re-layouts, per_device(): scores = own.astype(jnp.float32) + across.astype(jnp.float32)  27.8 us
    all_to_all x1, waiting for transfers between devices, mirrored(): lax.all_to_all(lax.all_to_all(regrouped, 'row', split_axis=0, concat_axis...  27.8 us
    dot_general x6, matrix products, backward_block(): jnp.dot(dhidden, w_expand.T, preferred_element_type=jnp.float32)  17.7 us
  transfers between devices with their start and end apart: 3, of which 3 were waited for; matrix products, arithmetic and copies ran while one was open for 2% of the time, Pallas kernels for 0%

profile of v1, /device:TPU:1, one launch (start us, length us, event | category | flops | bytes accessed | tf_op | source)
XLA Modules:
  0.0 587.4 jit_solution(5739879070008248552)
XLA Ops:
  7.3 138.0 %all-gather.3.cloned.1.call-done = bf16[64,192,256]{2,1,0:T(8,128)(2,1)} async-done(((bf16[2,192,256]{2,1,0:T(8,128)(2,1)}), bf16[64,192,256]{2,1,0:T(8,128)(2,1)}) %all-gather.3.cloned.1.call-update) | async-done | bytes 6291472 | tf_op jit(solution)/shard_map/all_gather | solution.py:57
  145.3 5.2 convert_reduce_fusion.2
  150.5 4.4 fusion.54
  155.0 5.2 fusion.60
  164.1 29.6 %all-gather.5.cloned.1.call-done = bf16[8,64,1536]{2,1,0:T(8,128)(2,1)} async-done(((bf16[1,64,1536]{2,1,0:T(8,128)(2,1)}), bf16[8,64,1536]{2,1,0:T(8,128)(2,1)}) %all-gather.5.cloned.1.call-update) | async-done | bytes 1572880 | tf_op jit(solution)/shard_map/all_gather | solution.py:14
  196.2 158.3 %while.24 = (s32[]{:T(128)}, bf16[6,1536,128]{1,2,0:T(8,128)(2,1)}, bf16[6,1536,512]{2,1,0:T(8,128)(2,1)}, bf16[6,8,12288]{2,1,0:T(8,128)(2,1)}, bf16[6,8,192,12...) while((s32[]{:T(128)}, bf16[6,1536,128]{1,2,0:T(8,128)(2,1)}, ...), condition=%wide.region_6.7_spmd, body=%wide.region_3.6_spmd.sunk | while | flops 1043695104 | bytes 37036208 | solution.py:99
  196.2 2.5 fusion.107
  198.7 4.5 copy.121
  203.2 6.3 %convert_element_type.286 = bf16[1536,1024]{0,1:T(8,128)(2,1)S(1)} reshape(bf16[8,192,32,32]{1,0,3,2:T(8,128)(2,1)} %copy.121) | data formatting | bytes 6291456 | tf_op jit(solution)/shard_map/while/body/eval_jaxpr/convert_element_type | solution.py:80
  211.5 2.3 copy.120
  213.8 2.6 bitcast_dynamic-update-slice_fusion.4
  217.8 2.3 convolution_convert_fusion.5
  222.6 2.5 fusion.107
  225.1 4.5 copy.121
  229.6 6.3 %convert_element_type.286 = bf16[1536,1024]{0,1:T(8,128)(2,1)S(1)} reshape(bf16[8,192,32,32]{1,0,3,2:T(8,128)(2,1)} %copy.121) | data formatting | bytes 6291456 | tf_op jit(solution)/shard_map/while/body/eval_jaxpr/convert_element_type | solution.py:80
  237.9 2.3 copy.120
  240.2 2.6 bitcast_dynamic-update-slice_fusion.4
  244.1 2.3 convolution_convert_fusion.5
  249.0 2.5 fusion.107
  251.5 4.5 copy.121
  256.0 6.3 %convert_element_type.286 = bf16[1536,1024]{0,1:T(8,128)(2,1)S(1)} reshape(bf16[8,192,32,32]{1,0,3,2:T(8,128)(2,1)} %copy.121) | data formatting | bytes 6291456 | tf_op jit(solution)/shard_map/while/body/eval_jaxpr/convert_element_type | solution.py:80
  264.3 2.3 copy.120
  266.6 2.6 bitcast_dynamic-update-slice_fusion.4
  270.5 2.3 convolution_convert_fusion.5
  275.4 2.5 fusion.107
  277.8 4.5 copy.121
  282.3 6.3 %convert_element_type.286 = bf16[1536,1024]{0,1:T(8,128)(2,1)S(1)} reshape(bf16[8,192,32,32]{1,0,3,2:T(8,128)(2,1)} %copy.121) | data formatting | bytes 6291456 | tf_op jit(solution)/shard_map/while/body/eval_jaxpr/convert_element_type | solution.py:80
  290.6 2.3 copy.120
  292.9 2.6 bitcast_dynamic-update-slice_fusion.4
  296.8 2.3 convolution_convert_fusion.5
  301.7 2.5 fusion.107
  304.2 4.5 copy.121
  308.7 6.3 %convert_element_type.286 = bf16[1536,1024]{0,1:T(8,128)(2,1)S(1)} reshape(bf16[8,192,32,32]{1,0,3,2:T(8,128)(2,1)} %copy.121) | data formatting | bytes 6291456 | tf_op jit(solution)/shard_map/while/body/eval_jaxpr/convert_element_type | solution.py:80
  317.0 2.3 copy.120
  319.3 2.5 bitcast_dynamic-update-slice_fusion.4
  323.2 2.3 convolution_convert_fusion.5
  328.1 2.5 fusion.107
  330.6 4.5 copy.121
  335.1 6.3 %convert_element_type.286 = bf16[1536,1024]{0,1:T(8,128)(2,1)S(1)} reshape(bf16[8,192,32,32]{1,0,3,2:T(8,128)(2,1)} %copy.121) | data formatting | bytes 6291456 | tf_op jit(solution)/shard_map/while/body/eval_jaxpr/convert_element_type | solution.py:80
  343.4 2.3 copy.120
  345.6 2.6 bitcast_dynamic-update-slice_fusion.4
  349.6 2.3 convolution_convert_fusion.5
  354.5 2.0 reshape_reshape.7
  356.5 34.0 %all_to_all.26 = bf16[8,4,6,3072]{3,1,2,0:T(4,128)(2,1)S(1)} all-to-all(bf16[8,4,6,3072]{3,1,2,0:T(4,128)(2,1)S(1)} %bitcast.141), channel_id=1, replica_groups=mesh['row'=32,'col'=8] {'col'}, dimensions={0} | all-to-all | bytes 2359296 | tf_op jit(solution)/shard_map/all_to_all | solution.py:36
  390.9 50.7 %all_to_all.27 = bf16[32,1,6,3072]{3,2,1,0:T(8,128)(2,1)} all-to-all(bf16[32,1,6,3072]{3,2,1,0:T(8,128)(2,1)S(1)} %bitcast.140), channel_id=1, replica_groups=mesh['row'=32,'col'=8] {'row'}, dimensions={0} | all-to-all | bytes 2359296 | tf_op jit(solution)/shard_map/all_to_all | solution.py:39
  441.6 7.7 %all-to-all-start.2 = ((bf16[1,32,6,3072]{3,2,0,1:T(8,128)(2,1)}), bf16[1,32,6,3072]{3,2,0,1:T(8,128)(2,1)}, u32[]{:S(2)}, u32[]{:S(2)}) async-start(bf16[1,32,6,3072]{3,2,0,1:T(8,128)(2,1)} %bitcast.21), calls=%async_computation.2 | async-start | bytes 3145728 | tf_op jit(solution)/shard_map/all_to_all | solution.py:38
  451.3 3.6 reshape.148
  454.9 3.5 reshape.146
  458.4 27.8 %all-to-all-done.2 = bf16[1,32,6,3072]{3,2,0,1:T(8,128)(2,1)} async-done(((bf16[1,32,6,3072]{3,2,0,1:T(8,128)(2,1)}), bf16[1,32,6,3072]{3,2,0,1:T(8,128)(2,1)}, u32[]{:S(2)}, u32[]{:S(2)}) %all-to-all-start.2) | async-done | bytes 1179680 | tf_op jit(solution)/shard_map/all_to_all | solution.py:38
  486.3 2.1 copy_convert_fusion
  488.4 3.2 reshape.150
  491.6 3.0 copy.100
  495.3 2.4 fusion.63
  497.7 4.7 exponential_reduce_fusion
  502.5 7.9 %copy.99 = f32[48,4,8,6,64]{4,3,2,1,0:T(8,128)} copy(f32[48,4,8,6,64]{4,0,1,2,3:T(8,128)} %bitcast.139) | data formatting | bytes 4718592 | tf_op jit(solution)/shard_map/convert_element_type | solution.py:104
  510.4 6.6 %reshape.147 = f32[6,1536,64]{2,1,0:T(8,128)} reshape(f32[48,4,8,6,64]{4,3,2,1,0:T(8,128)} %copy.99) | data formatting | bytes 4718592 | tf_op jit(solution)/shard_map/convert_element_type | solution.py:104
  517.1 8.4 %multiply_convert_fusion.1 = bf16[6,1536,64]{2,1,0:T(8,128)(2,1)} fusion(f32[6,1536,64]{2,1,0:T(8,128)} %reshape.146, f32[6,1536,64]{2,1,0:T(8,128)} %reshape.147, f32[6,1536]{1,0:T(8,128)S(1)} %multiply_multiply_fusion, s32[6,1536]{1,0:T(8,128)S(1)} %eq.22, f32[6,1536]{1,0:T(8,128)S(1)} %div.58, f32[6,1536]{1,0:T(8,128)S(1)} %sub.64), kind=kLoop, calls=%fused_computation.82 | loop fusion | flops 4718592 | bytes 6045696 | tf_op jit(solution)/shard_map/convert_element_type | solution.py:116
  525.5 54.4 %while.25 = (s32[]{:T(128)}, bf16[6,1536,128]{2,1,0:T(8,128)(2,1)}, bf16[6,1536,64]{2,1,0:T(8,128)(2,1)}, bf16[128,64]{0,1:T(8,128)(2,1)S(1)}, bf16[6,1536,128]{...) while((s32[]{:T(128)}, bf16[6,1536,128]{2,1,0:T(8,128)(2,1)}, ...), condition=%wide.region_14.15_spmd, body=%wide.region_9.14_spmd.sunk | while | flops 440010240 | bytes 12193377 | solution.py:143
  528.9 2.9 fusion.115
  537.9 3.0 fusion.115
  547.0 2.9 fusion.115
  556.0 3.0 fusion.115
  565.0 2.9 fusion.115
  574.0 3.0 fusion.115
  (208 shorter events, 82.4 us)
Async XLA Ops:
  6.5 148.5 %copy-start = (bf16[256,64]{0,1:T(8,128)(2,1)S(1)}, bf16[256,64]{0,1:T(8,128)(2,1)}, u32[]{:S(2)}) copy-start(bf16[256,64]{0,1:T(8,128)(2,1)} %param.17) | copy-start | bytes 98308
  6.5 138.8 %all-gather.3.cloned.1.call-start = ((), (), s32[]{:S(2)}) async-start(), calls=%async_computation.3 | async-start | bytes 6488064 | tf_op jit(solution)/shard_map/all_gather | solution.py:57
  7.3 186.4 %all-gather.5.cloned.1.call-start = ((), (), s32[]{:S(2)}) async-start(), calls=%async_computation.4 | async-start | bytes 1769472 | tf_op jit(solution)/shard_map/all_gather | solution.py:14
  145.3 5.2 copy-start.3
  160.7 35.6 %copy-start.5 = (bf16[1024,128]{1,0:T(8,128)(2,1)S(1)}, bf16[1024,128]{1,0:T(8,128)(2,1)}, u32[]{:S(2)}) copy-start(bf16[1024,128]{1,0:T(8,128)(2,1)} %param.18) | copy-start | bytes 786436
  160.7 35.6 %copy-start.8 = (bf16[128,64]{0,1:T(8,128)(2,1)S(1)}, bf16[128,64]{0,1:T(8,128)(2,1)}, u32[]{:S(2)}) copy-start(bf16[128,64]{0,1:T(8,128)(2,1)} %param.21) | copy-start | bytes 49156
  213.8 3.3 copy-start.6
  216.4 0.7 copy-start.2
  240.2 3.3 copy-start.6
  242.8 0.7 copy-start.2
  266.6 3.3 copy-start.6
  269.1 0.7 copy-start.2
  292.9 3.3 copy-start.6
  295.5 0.7 copy-start.2
  319.3 3.3 copy-start.6
  321.9 0.7 copy-start.2
  345.6 3.3 copy-start.6
  348.2 0.7 copy-start.2
  390.9 60.3 %copy-start.9 = (s32[48,192]{1,0:T(8,128)S(1)}, s32[48,192]{1,0:T(8,128)}, u32[]{:S(2)}) copy-start(s32[48,192]{1,0:T(8,128)} %param.15) | copy-start | bytes 110596
  390.9 60.4 %copy-start.4 = (bf16[6,8,12288]{2,1,0:T(8,128)(2,1)S(1)}, bf16[6,8,12288]{2,1,0:T(8,128)(2,1)}, u32[]{:S(2)}) copy-start(bf16[6,8,12288]{2,1,0:T(8,128)(2,1)} %get-tuple-element.106) | copy-start | bytes 3538948
  441.6 44.7 %all-to-all-start.2 = ((bf16[1,32,6,3072]{3,2,0,1:T(8,128)(2,1)}), bf16[1,32,6,3072]{3,2,0,1:T(8,128)(2,1)}, u32[]{:S(2)}, u32[]{:S(2)}) async-start(bf16[1,32,6,3072]{3,2,0,1:T(8,128)(2,1)} %bitcast.21), calls=%async_computation.2 | async-start | bytes 3145728 | tf_op jit(solution)/shard_map/all_to_all | solution.py:38
  491.5 3.6 slice-start
  491.5 3.7 slice-start.1
  517.0 8.4 %copy-start.7 = (bf16[128,512]{1,0:T(8,128)(2,1)S(1)}, bf16[128,512]{1,0:T(8,128)(2,1)}, u32[]{:S(2)}) copy-start(bf16[128,512]{1,0:T(8,128)(2,1)} %get-tuple-element.464) | copy-start | bytes 393220
  517.1 8.4 %copy-start.10 = (bf16[512,128]{1,0:T(8,128)(2,1)S(1)}, bf16[512,128]{1,0:T(8,128)(2,1)}, u32[]{:S(2)}) copy-start(bf16[512,128]{1,0:T(8,128)(2,1)} %get-tuple-element.471) | copy-start | bytes 393220
  579.8 0.8 copy-start.1
Sparse Core Ops, SparseCore 0:
  10.8 134.4 all-gather.2
  162.6 30.9 all-gather.4
